TPU v7x, 256 devices: a whole 4x4x8 slice. The times are simulated.
256 devices in a mesh: gx: 4 (over y), gy: 16 (over z, core), gz: 4 (over x).
Axes of the slice: x: 4, y: 4, z: 8, core: 2. Of those that a mesh axis runs over, the one named last changes fastest.
Arguments:
- flux_jacobian_factor: bfloat16 [4, 64, 8, 320, 320], P('gx', 'gy', 'gz'), may hold values from -6 to 6
- mass_over_timestep: float32 [4, 64, 8, 320], P('gx', 'gy', 'gz'), may hold values from 0.5 to 2
- face_jacobian: float32 [4, 64, 8, 3, 80, 160], P('gx', 'gy', 'gz'), may hold values from -1 to 1
- face_flags: int32 [4, 64, 8, 6], P('gx', 'gy', 'gz'), may hold values from 0 to 1, as said below
- right_side: float32 [4, 64, 8, 320], P('gx', 'gy', 'gz'), may hold values from -36 to 36
Outputs:
- update: float32 [4, 64, 8, 320], P('gx', 'gy', 'gz')
Inputs may be any that keep to these rules, and one draw needn't show every extreme that they name: face_flags[e, 2 d] and face_flags[e, 2 d + 1] mark the lower and upper face of element e along dimension d as a wall (1) or open (0); the upper flag of an element along a dimension equals the lower flag of the element after it along that dimension.
All inputs are finite; a program needn't handle non-finite values.
Results may differ from a plain program's by a relative error of at most 0.0003.
Values sent between devices are 32-bit elements; how exact they have to be, the bound alone decides.
No kernel may reach another device: no remote copies, remote signals or barrier semaphores. Data moves between devices by JAX's collectives and lax.ppermute only.
A program may use at most 128 MiB of HBM per device.

v0:
```python
import jax
import jax.numpy as jnp
from jax import lax
from jax.sharding import PartitionSpec as P

VARS = 5
ORDER = 4
KRYLOV = 3
ELEMENT_UNKNOWNS = 320
FACE_UNKNOWNS = 80


full_precision = lax.Precision.HIGHEST
wall_weight = 0.5


def passed_along(block, axis, distance):
    devices = range(lax.axis_size(axis))
    route = [(i - distance, i) for i in devices if i - distance in devices]
    return lax.ppermute(block, axis, route)


def padded_2(cells, sides, width):
    for axis, dim in sides:
        count = lax.axis_size(axis)
        ends = count - 1
        head = lax.slice_in_dim(cells, 0, width, axis=dim)
        tail = lax.slice_in_dim(cells, cells.shape[dim] - width, cells.shape[dim], axis=dim)
        cells = jnp.concatenate(
            [
                lax.ppermute(tail, axis, [(i, (i + 1) % count) for i in range(ends)]),
                cells,
                lax.ppermute(head, axis, [((i + 1) % count, i) for i in range(ends)]),
            ],
            axis=dim,
        )
    return cells


def take_face(field, d, index):
    lead = field.shape[:3]
    cube = field.reshape(lead + (VARS, ORDER, ORDER, ORDER))
    face = lax.index_in_dim(cube, index, axis=4 + d, keepdims=False)
    return face.reshape(lead + (FACE_UNKNOWNS,))


def put_face(values, d, index):
    lead = values.shape[:3]
    cube = jnp.zeros(lead + (VARS, ORDER, ORDER, ORDER), values.dtype)
    spot = (slice(None),) * (4 + d) + (index,)
    cube = cube.at[spot].set(values.reshape(lead + (VARS, ORDER, ORDER)))
    return cube.reshape(lead + (ELEMENT_UNKNOWNS,))


def face_flux(matrix, left_trace, right_trace):
    paired = jnp.concatenate([left_trace, right_trace], axis=-1)
    return jnp.einsum("abcfg,abcg->abcf", matrix, paired, precision=full_precision)


def couple_faces(field, d, w_dim, face_flags, below_trace, top_flux):
    count = field.shape[d]
    lower_trace = take_face(field, d, 0)
    upper_trace = take_face(field, d, ORDER - 1)
    lower_flux = face_flux(w_dim, below_trace, lower_trace)
    upper_flux = jnp.concatenate(
        [lax.slice_in_dim(lower_flux, 1, count, axis=d), top_flux(lower_flux, upper_trace)], axis=d
    )
    lower_open = (1 - face_flags[..., 2 * d : 2 * d + 1]).astype(jnp.float32)
    upper_open = (1 - face_flags[..., 2 * d + 1 : 2 * d + 2]).astype(jnp.float32)
    lower_part = -lower_open * lower_flux + (1.0 - lower_open) * wall_weight * lower_trace
    upper_part = upper_open * upper_flux + (1.0 - upper_open) * wall_weight * upper_trace
    return put_face(lower_part, d, 0) + put_face(upper_part, d, ORDER - 1)


def neighbour(padded, d, start, length):
    spots = []
    for axis_pos in range(3):
        if axis_pos == d:
            spots.append(slice(start, start + length))
        else:
            spots.append(slice(1, padded.shape[axis_pos] - 1))
    return padded[tuple(spots)]


def ghost_faces(field, padded, d, w_dim, w_top, face_flags):
    count = field.shape[d]
    below_trace = take_face(neighbour(padded, d, 0, count), d, ORDER - 1)
    above_top = take_face(neighbour(padded, d, count + 1, 1), d, 0)

    def top_flux(lower_flux, upper_trace):
        return face_flux(w_top, lax.slice_in_dim(upper_trace, count - 1, count, axis=d), above_top)

    return couple_faces(field, d, w_dim, face_flags, below_trace, top_flux)


def least_squares(columns, start_norm):
    count = len(columns)
    cosines = []
    sine_terms = []
    target_values = [start_norm] + [jnp.zeros((), jnp.float32) for i in range(count)]
    triangle = []
    for j in range(count):
        column = list(columns[j])
        for i in range(j):
            first_entry = column[i]
            second_entry = column[i + 1]
            column[i] = cosines[i] * first_entry + sine_terms[i] * second_entry
            column[i + 1] = -sine_terms[i] * first_entry + cosines[i] * second_entry
        radius = jnp.sqrt(column[j] * column[j] + column[j + 1] * column[j + 1])
        cosine = column[j] / radius
        sine_part = column[j + 1] / radius
        cosines.append(cosine)
        sine_terms.append(sine_part)
        column[j] = radius
        target_values[j + 1] = -sine_part * target_values[j]
        target_values[j] = cosine * target_values[j]
        triangle.append(column[: j + 1])
    weights = [None] * count
    for i in reversed(range(count)):
        running = target_values[i]
        for k in range(i + 1, count):
            running = running - triangle[k][i] * weights[k]
        weights[i] = running / triangle[i][i]
    return weights


def precond_apply(precond, vector):
    return jnp.einsum("abcij,abcj->abci", precond, vector, precision=full_precision)


def shards(flux_jacobian_factor, mass_over_timestep, face_jacobian, face_flags, right_side):
    gram_part = jnp.einsum(
        "abcki,abckj->abcij",
        flux_jacobian_factor,
        flux_jacobian_factor,
        preferred_element_type=jnp.float32,
    )
    identity = jnp.eye(ELEMENT_UNKNOWNS, dtype=jnp.float32)
    jacobian = gram_part / ELEMENT_UNKNOWNS + mass_over_timestep[..., None] * identity
    factor_lower = jnp.linalg.cholesky(jacobian)
    lower_inverse = jax.scipy.linalg.solve_triangular(
        factor_lower, jnp.broadcast_to(identity, jacobian.shape), lower=True
    )
    precond = jnp.einsum(
        "abcki,abckj->abcij", lower_inverse, lower_inverse, precision=full_precision
    )
    top_blocks = (
        passed_along(face_jacobian[0:1, :, :, 0], "gx", -1),
        passed_along(face_jacobian[:, 0:1, :, 1], "gy", -1),
        passed_along(face_jacobian[:, :, 0:1, 2], "gz", -1),
    )
    start_norm = jnp.sqrt(lax.psum(jnp.sum(right_side * right_side), ("gx", "gy", "gz")))
    krylov_basis = [right_side / start_norm]
    columns = []
    for j in range(KRYLOV):
        direction = precond_apply(precond, krylov_basis[j])
        mapped = jnp.einsum("abcij,abcj->abci", jacobian, direction, precision=full_precision)
        padded = padded_2(direction, (("gx", 0), ("gy", 1), ("gz", 2)), 1)
        for d in range(3):
            mapped = mapped + ghost_faces(
                direction, padded, d, face_jacobian[:, :, :, d], top_blocks[d], face_flags
            )
        local_dots = jnp.stack([jnp.sum(vector * mapped) for vector in krylov_basis])
        project = lax.psum(local_dots, ("gx", "gy", "gz"))
        for i in range(len(krylov_basis)):
            mapped = mapped - project[i] * krylov_basis[i]
        length = jnp.sqrt(lax.psum(jnp.sum(mapped * mapped), ("gx", "gy", "gz")))
        columns.append([project[i] for i in range(len(krylov_basis))] + [length])
        if j + 1 < KRYLOV:
            krylov_basis.append(mapped / length)
    weights = least_squares(columns, start_norm)
    combined = weights[0] * krylov_basis[0]
    for j in range(1, KRYLOV):
        combined = combined + weights[j] * krylov_basis[j]
    return precond_apply(precond, combined)


def solution(mesh):
    in_specs = (
        P("gx", "gy", "gz", None, None),
        P("gx", "gy", "gz", None),
        P("gx", "gy", "gz", None, None, None),
        P("gx", "gy", "gz", None),
        P("gx", "gy", "gz", None),
    )
    out_specs = P("gx", "gy", "gz", None)
    return jax.shard_map(shards, mesh=mesh, in_specs=in_specs, out_specs=out_specs, check_vma=False)
```

profile of v0, /device:TPU:1, one launch (start us, length us, event | category | flops | bytes accessed | tf_op | source)
XLA Modules:
  0.0 1564.7 jit_solution(18332297160623081579)
XLA Ops:
  6.0 5.4 copy.356
  17.0 93.8 %custom-call.26 = f32[1,4,2,128,128]{4,3,2,1,0:T(8,128)S(1)} custom-call(f32[1,4,2,128,128]{4,3,2,1,0:T(8,128)S(1)} %cholesky.211), custom_call_target="Cholesky" | custom-call | tf_op jit(solution)/shard_map/jit(cholesky)/cholesky | solution.py:140
  110.9 78.6 %custom-call.27 = f32[1,4,2,1,128,128]{4,5,3,2,1,0:T(8,128)S(1)} custom-call(f32[1,4,2,1,128,128]{5,4,3,2,1,0:T(8,128)S(1)} %select_bitcast_fusion.1), custom_call_target="InvertDiagBlocksLowerTriangular" | custom-call | tf_op jit(solution)/shard_map/jit(cholesky)/cholesky | solution.py:140
  197.2 94.0 %custom-call.28 = f32[1,4,2,128,128]{4,3,2,1,0:T(8,128)S(1)} custom-call(f32[1,4,2,128,128]{4,3,2,1,0:T(8,128)S(1)} %cholesky.215), custom_call_target="Cholesky" | custom-call | tf_op jit(solution)/shard_map/jit(cholesky)/cholesky | solution.py:140
  292.2 78.6 %custom-call.29 = f32[1,4,2,1,128,128]{4,5,3,2,1,0:T(8,128)S(1)} custom-call(f32[1,4,2,1,128,128]{5,4,3,2,1,0:T(8,128)S(1)} %get-tuple-element.264), custom_call_target="InvertDiagBlocksLowerTriangular" | custom-call | tf_op jit(solution)/shard_map/jit(cholesky)/cholesky | solution.py:140
  374.0 46.9 %custom-call.30 = f32[1,4,2,64,64]{4,3,2,1,0:T(8,128)S(1)} custom-call(f32[1,4,2,64,64]{4,3,2,1,0:T(8,128)S(1)} %fusion.17), custom_call_target="Cholesky" | custom-call | tf_op jit(solution)/shard_map/jit(cholesky)/cholesky | solution.py:140
  427.1 8.4 while.19
  437.0 236.9 %custom-call.31 = f32[4,2,3,128,128]{3,4,2,1,0:T(8,128)} custom-call(f32[4,2,3,128,128]{4,3,2,1,0:T(8,128)S(1)} %pad_maximum_fusion), custom_call_target="InvertDiagBlocksLowerTriangular" | custom-call | tf_op jit(solution)/shard_map/jit(_solve_triangular)/vmap(vmap())/triangular_solve | solution.py:141
  688.3 10.2 fusion
  698.5 81.4 %psum.49 = f32[]{:T(128)} all-reduce(f32[]{:T(128)} %multiply_reduce_fusion.2), channel_id=1, replica_groups=mesh['gx'=4,'gy'=16,'gz'=4] {'gx','gy','gz'}, use_global_device_ids=true, to_apply=%region_7.8 | all-reduce | flops 1 | bytes 8 | tf_op jit(solution)/shard_map/psum | solution.py:152
  780.5 5.7 fusion.108
  813.4 4.9 fusion.106
  867.2 4.9 collective-permute-start.6
  911.7 78.9 %psum.50 = f32[]{:T(128)} all-reduce(f32[]{:T(128)} %get-tuple-element.260), channel_id=1, replica_groups=mesh['gx'=4,'gy'=16,'gz'=4] {'gx','gy','gz'}, use_global_device_ids=true, to_apply=%region_9.10 | all-reduce | flops 1 | bytes 8 | tf_op jit(solution)/shard_map/psum | solution.py:164
  991.8 72.8 %psum.51 = f32[]{:T(128)} all-reduce(f32[]{:T(128)} %multiply_reduce_fusion.1), channel_id=1, replica_groups=mesh['gx'=4,'gy'=16,'gz'=4] {'gx','gy','gz'}, use_global_device_ids=true, to_apply=%region_11.12 | all-reduce | flops 1 | bytes 8 | tf_op jit(solution)/shard_map/psum | solution.py:167
  1066.0 5.7 fusion.104
  1080.1 4.9 fusion.102
  1166.2 77.7 %psum.52 = f32[2]{0:T(128)S(1)} all-reduce(f32[2]{0:T(128)S(1)} %pad_maximum_fusion.37), channel_id=1, replica_groups=mesh['gx'=4,'gy'=16,'gz'=4] {'gx','gy','gz'}, use_global_device_ids=true, to_apply=%region_14.15 | all-reduce | flops 2 | bytes 16 | tf_op jit(solution)/shard_map/psum | solution.py:164
  1246.3 72.7 %psum.53 = f32[]{:T(128)} all-reduce(f32[]{:T(128)} %get-tuple-element.257), channel_id=1, replica_groups=mesh['gx'=4,'gy'=16,'gz'=4] {'gx','gy','gz'}, use_global_device_ids=true, to_apply=%region_16.17 | all-reduce | flops 1 | bytes 8 | tf_op jit(solution)/shard_map/psum | solution.py:167
  1319.7 5.7 fusion.100
  1333.6 4.9 fusion.98
  1398.8 78.6 %psum.54 = f32[3]{0:T(128)S(1)} all-reduce(f32[3]{0:T(128)S(1)} %pad_maximum_fusion.38), channel_id=1, replica_groups=mesh['gx'=4,'gy'=16,'gz'=4] {'gx','gy','gz'}, use_global_device_ids=true, to_apply=%region_20.21 | all-reduce | flops 3 | bytes 24 | tf_op jit(solution)/shard_map/psum | solution.py:164
  1484.3 72.6 %psum.55 = f32[]{:T(128)} all-reduce(f32[]{:T(128)} %fusion.110), channel_id=1, replica_groups=mesh['gx'=4,'gy'=16,'gz'=4] {'gx','gy','gz'}, use_global_device_ids=true, to_apply=%region_22.23 | all-reduce | flops 1 | bytes 8 | tf_op jit(solution)/shard_map/psum | solution.py:167
  1557.9 5.7 fusion.96
  (426 shorter events, 330.2 us)
Async XLA Ops:
  427.1 247.0 %copy-start.8 = (f32[128,320]{0,1:T(8,128)S(1)}, f32[128,320]{0,1:T(8,128)}, u32[]{:S(2)}) copy-start(f32[128,320]{0,1:T(8,128)} %get-tuple-element.267) | copy-start | bytes 491524
  435.4 240.8 %copy-start.7 = (f32[128,320]{0,1:T(8,128)S(1)}, f32[128,320]{0,1:T(8,128)}, u32[]{:S(2)}) copy-start(f32[128,320]{0,1:T(8,128)} %get-tuple-element.266) | copy-start | bytes 491524
  786.2 61.6 %collective-permute-start = (f32[1,4,2,320]{3,1,2,0:T(4,128)S(1)}, f32[1,4,2,320]{3,1,2,0:T(4,128)}, u32[]{:S(2)}, u32[]{:S(2)}) collective-permute-start(f32[1,4,2,320]{3,1,2,0:T(4,128)S(1)} %bitcast.397), channel_id=1, source_target_pairs={{0,64},{64,128},{128,192},{1,65},{65,129},{129,193},{2,66},{66,130... | collective-permute-start | bytes 30728 | tf_op jit(solution)/shard_map/ppermute | solution.py:31
  788.1 65.2 %collective-permute-start.1 = (f32[1,4,2,320]{3,1,2,0:T(4,128)S(1)}, f32[1,4,2,320]{3,1,2,0:T(4,128)}, u32[]{:S(2)}, u32[]{:S(2)}) collective-permute-start(f32[1,4,2,320]{3,1,2,0:T(4,128)S(1)} %bitcast.398), channel_id=1, source_target_pairs={{64,0},{128,64},{192,128},{65,1},{129,65},{193,129},{66,2},{130,66... | collective-permute-start | bytes 30728 | tf_op jit(solution)/shard_map/ppermute | solution.py:33
  790.3 117.2 %collective-permute-start.2 = (f32[1,4,2,80,160]{4,3,2,1,0:T(8,128)}, f32[1,4,2,80,160]{4,3,2,1,0:T(8,128)S(1)}, u32[]{:S(2)}, u32[]{:S(2)}) collective-permute-start(f32[1,4,2,80,160]{4,3,2,1,0:T(8,128)} %slice_bitcast_fusion.2), channel_id=1, source_target_pairs={{64,0},{128,64},{192,128},{65,1},{129,65},{193,129},{66,2},{130,66... | collective-permute-start | bytes 1228808 | tf_op jit(solution)/shard_map/ppermute | solution.py:20
  792.3 103.3 %collective-permute-start.5 = (f32[1,1,2,80,160]{4,3,2,1,0:T(8,128)}, f32[1,1,2,80,160]{4,3,2,1,0:T(8,128)S(1)}, u32[]{:S(2)}, u32[]{:S(2)}) collective-permute-start(f32[1,1,2,80,160]{4,3,2,1,0:T(8,128)} %slice_bitcast_fusion.16), channel_id=1, source_target_pairs={{4,0},{8,4},{12,8},{16,12},{20,16},{24,20},{28,24},{32,28},{36,32}... | collective-permute-start | bytes 307208 | tf_op jit(solution)/shard_map/ppermute | solution.py:20
  795.9 107.2 %collective-permute-start.8 = (f32[1,4,1,80,160]{4,3,1,2,0:T(8,128)}, f32[1,4,1,80,160]{4,3,1,2,0:T(8,128)S(1)}, u32[]{:S(2)}, u32[]{:S(2)}) collective-permute-start(f32[1,4,1,80,160]{4,3,1,2,0:T(8,128)} %slice_bitcast_fusion.11), channel_id=1, source_target_pairs={{1,0},{2,1},{3,2},{5,4},{6,5},{7,6},{9,8},{10,9},{11,10},{13,12},{... | collective-permute-start | bytes 614408 | tf_op jit(solution)/shard_map/ppermute | solution.py:20
  857.6 7.6 collective-permute-start.3
  860.4 5.4 collective-permute-start.4
  867.2 11.3 collective-permute-start.6
  875.7 16.5 %collective-permute-start.7 = (f32[3,6,1,320]{3,1,2,0:T(8,128)}, f32[3,6,1,320]{3,1,2,0:T(8,128)}, u32[]{:S(2)}, u32[]{:S(2)}) collective-permute-start(f32[3,6,1,320]{3,1,2,0:T(8,128)} %get-tuple-element.287), channel_id=1, source_target_pairs={{1,0},{2,1},{3,2},{5,4},{6,5},{7,6},{9,8},{10,9},{11,10},{13,12},{... | collective-permute-start | bytes 69128 | tf_op jit(solution)/shard_map/ppermute | solution.py:33
  1072.3 28.7 %collective-permute-start.9 = (f32[1,4,2,320]{3,1,2,0:T(4,128)}, f32[1,4,2,320]{3,1,2,0:T(4,128)}, u32[]{:S(2)}, u32[]{:S(2)}) collective-permute-start(f32[1,4,2,320]{3,1,2,0:T(4,128)} %bitcast.312.clone.2), channel_id=1, source_target_pairs={{0,64},{64,128},{128,192},{1,65},{65,129},{129,193},{2,66},{66,130... | collective-permute-start | bytes 30728 | tf_op jit(solution)/shard_map/ppermute | solution.py:31
  1075.5 31.8 %collective-permute-start.10 = (f32[1,4,2,320]{3,1,2,0:T(4,128)}, f32[1,4,2,320]{3,1,2,0:T(4,128)}, u32[]{:S(2)}, u32[]{:S(2)}) collective-permute-start(f32[1,4,2,320]{3,1,2,0:T(4,128)} %bitcast.312.clone.2), channel_id=1, source_target_pairs={{64,0},{128,64},{192,128},{65,1},{129,65},{193,129},{66,2},{130,66... | collective-permute-start | bytes 30728 | tf_op jit(solution)/shard_map/ppermute | solution.py:33
  1115.7 9.2 collective-permute-start.11
  1119.4 5.5 collective-permute-start.12
  1126.3 9.2 collective-permute-start.13
  1134.0 23.4 %collective-permute-start.14 = (f32[3,6,1,320]{3,1,2,0:T(8,128)}, f32[3,6,1,320]{3,1,2,0:T(8,128)}, u32[]{:S(2)}, u32[]{:S(2)}) collective-permute-start(f32[3,6,1,320]{3,1,2,0:T(8,128)} %get-tuple-element.285), channel_id=1, source_target_pairs={{1,0},{2,1},{3,2},{5,4},{6,5},{7,6},{9,8},{10,9},{11,10},{13,12},{... | collective-permute-start | bytes 69128 | tf_op jit(solution)/shard_map/ppermute | solution.py:33
  1326.0 28.9 %collective-permute-start.15 = (f32[1,4,2,320]{3,1,2,0:T(4,128)}, f32[1,4,2,320]{3,1,2,0:T(4,128)}, u32[]{:S(2)}, u32[]{:S(2)}) collective-permute-start(f32[1,4,2,320]{3,1,2,0:T(4,128)} %bitcast.309.clone.2), channel_id=1, source_target_pairs={{0,64},{64,128},{128,192},{1,65},{65,129},{129,193},{2,66},{66,130... | collective-permute-start | bytes 30728 | tf_op jit(solution)/shard_map/ppermute | solution.py:31
  1329.2 32.0 %collective-permute-start.16 = (f32[1,4,2,320]{3,1,2,0:T(4,128)}, f32[1,4,2,320]{3,1,2,0:T(4,128)}, u32[]{:S(2)}, u32[]{:S(2)}) collective-permute-start(f32[1,4,2,320]{3,1,2,0:T(4,128)} %bitcast.309.clone.2), channel_id=1, source_target_pairs={{64,0},{128,64},{192,128},{65,1},{129,65},{193,129},{66,2},{130,66... | collective-permute-start | bytes 30728 | tf_op jit(solution)/shard_map/ppermute | solution.py:33
  1368.4 7.9 collective-permute-start.17
  1372.4 5.3 collective-permute-start.18
  1378.5 4.9 collective-permute-start.19
  1381.9 10.9 collective-permute-start.20
  1391.9 172.3 %copy-start.1 = (bf16[1,4,2,320,320]{4,3,2,1,0:T(8,128)(2,1)S(1)}, bf16[1,4,2,320,320]{4,3,2,1,0:T(8,128)(2,1)}, u32[]{:S(2)}) copy-start(bf16[1,4,2,320,320]{4,3,2,1,0:T(8,128)(2,1)} %param.41) | copy-start | bytes 4915204
  (24 other events, 642.3 us)
where the time goes:
time: 1580 us; the launch traced here: 1560 us
  other arithmetic  709 us (45%)
  blocking collectives  535 us (34%)
  local copies, waits for them, and re-layouts  171 us (11%)
  matrix products  87.4 us (6%)
  starting transfers between devices  47.4 us (3%)
    another operation x14, other arithmetic, shards(): factor_lower = jnp.linalg.cholesky(jacobian)  394 us
    another operation x8, other arithmetic, shards(): jax.scipy.linalg.solve_triangular(factor_lower, jnp.broadcast_to(identity...  241 us
    psum x3, blocking collectives, shards(): project = lax.psum(local_dots, ('gx', 'gy', 'gz'))  235 us
    psum x3, blocking collectives, shards(): length = jnp.sqrt(lax.psum(jnp.sum(mapped * mapped), ('gx', 'gy', 'gz')))  218 us
    psum x1, blocking collectives, shards(): lax.psum(jnp.sum(right_side * right_side), ('gx', 'gy', 'gz'))  81.4 us
    another operation x48, local copies, waits for them, and re-layouts, take_face(): return face.reshape(lead + (FACE_UNKNOWNS,))  43.4 us
  transfers between devices with their start and end apart: 21, of which 1 were waited for; matrix products, arithmetic and copies ran while one was open for 13% of the time, Pallas kernels for 0%

commit v1 on v0

v1 whole, which is shorter than its diff:
```python
import jax
import jax.numpy as jnp
import numpy as np
from jax import lax
from jax.experimental import pallas as pl
from jax.experimental.pallas import tpu as pltpu
from jax.sharding import PartitionSpec as P

VARS = 5
ORDER = 4
KRYLOV = 3
UNKNOWNS = 320
FACE = 80
HEAD = 128
TAIL = UNKNOWNS - HEAD
CELLS = 8
LANES = 128
CONDITION_LIMIT = 40.0
wall_weight = 0.5

f32 = jnp.float32
bf16 = jnp.bfloat16
AXES = ("gx", "gy", "gz")


def face_nodes():
    cube = np.arange(UNKNOWNS).reshape(VARS, ORDER, ORDER, ORDER)
    nodes = []
    for d in range(3):
        for index in (0, ORDER - 1):
            nodes.append(np.take(cube, index, axis=1 + d).reshape(-1))
    return nodes


def gather_matrix():
    table = np.zeros((UNKNOWNS, 3 * 384), np.float32)
    nodes = face_nodes()
    for d in range(3):
        for k in range(FACE):
            table[nodes[2 * d + 1][k], 384 * d + k] = 1.0
            table[nodes[2 * d][k], 384 * d + LANES + FACE + k] = 1.0
    return table


def scatter_matrix():
    table = np.zeros((UNKNOWNS, 6 * FACE), np.float32)
    for side, nodes in enumerate(face_nodes()):
        for k in range(FACE):
            table[nodes[k], FACE * side + k] = 1.0
    return table


def wall_table():
    table = np.zeros((6, UNKNOWNS), np.float32)
    for side, nodes in enumerate(face_nodes()):
        table[side, nodes] = 1.0
    return table


def dot(a, b):
    return jnp.dot(a, b, preferred_element_type=f32)


def dot_nt(a, b):
    return lax.dot_general(a, b, (((1,), (1,)), ((), ())), preferred_element_type=f32)


def halves(a):
    high = a.astype(bf16)
    return high, (a - high.astype(f32)).astype(bf16)


def thirds(a):
    high = a.astype(bf16)
    rest = a - high.astype(f32)
    middle = rest.astype(bf16)
    return high, middle, (rest - middle.astype(f32)).astype(bf16)


def dot_split(a, b, product=dot):
    return product(a[0], b[0]) + (product(a[0], b[1]) + product(a[1], b[0]))


def eye_mask(n):
    rows = lax.broadcasted_iota(jnp.int32, (n, n), 0)
    cols = lax.broadcasted_iota(jnp.int32, (n, n), 1)
    return rows == cols


def approximate_inverses(blocks, lows):
    n = blocks[0].shape[0]
    diagonal = eye_mask(n)
    identity = jnp.where(diagonal, 1.0, 0.0)
    parts = [halves(a) for a in blocks]
    squares = [dot(p[0], p[0]) for p in parts]
    starts, errors, ratios = [], [], []
    for a, square, low in zip(blocks, squares, lows):
        sums = jnp.sum(jnp.abs(square), axis=0, keepdims=True)
        high = 1.03 * jnp.sqrt(jnp.max(sums, axis=1, keepdims=True))
        high = jnp.maximum(high, 1.1 * low)
        ratios.append(high / low)
        half = 0.5 * (high - low)
        mid = 0.5 * (high + low)
        inverse_half = 1.0 / half
        t = -mid * inverse_half
        t2 = t * t
        c3 = 16.0 * t
        c2 = 16.0 * t2 - 20.0
        c1 = t * c2
        c0 = t2 * c2 + 5.0
        top = t * c0
        gain = -inverse_half / top
        shifted = inverse_half * a + t * identity
        second = (inverse_half * inverse_half) * square + (2.0 * t) * shifted - t2 * identity
        inner = c3 * shifted + 16.0 * second
        outer = c1 * shifted + c2 * second + c0 * identity
        starts.append((second.astype(bf16), inner.astype(bf16), outer, gain))
        errors.append(1.0 / (top * top))
    firsts = [gain * (outer + dot(second, inner)) for second, inner, outer, gain in starts]
    narrow = [x.astype(bf16) for x in firsts]
    defects = [2.0 * identity - dot(p[0], x) for p, x in zip(parts, narrow)]
    seconds = [
        (2.0 / (2.0 - error)) * dot(x, e.astype(bf16))
        for x, e, error in zip(narrow, defects, errors)
    ]
    wide = [halves(x) for x in seconds]
    rests = [identity - dot_split(p, x) for p, x in zip(parts, wide)]
    small = [r.astype(bf16) for r in rests]
    sums = [r + dot(s, s) for r, s in zip(rests, small)]
    inverses = [
        x + dot_split(w, halves(s)) for x, w, s in zip(seconds, wide, sums)
    ]
    return inverses, ratios


def traces_of(field, gather):
    high, middle, low = thirds(field)
    stacked = jnp.concatenate([high.astype(f32), middle.astype(f32), low.astype(f32)], axis=0)
    out = dot(stacked.astype(bf16), gather)
    return out[0:8] + (out[8:16] + out[16:24])


def store_traces(traces, refs):
    for d in range(3):
        refs[2 * d][...] = traces[:, 384 * d : 384 * d + LANES]
        refs[2 * d + 1][...] = traces[:, 384 * d + LANES : 384 * (d + 1)]


def apply_inverses(inverse_ref, columns):
    rows = []
    for e in range(CELLS):
        rows.append(jnp.sum(inverse_ref[e] * columns[:, e : e + 1], axis=0, keepdims=True))
    return jnp.concatenate(rows, axis=0)


def invert_kernel(
    factor_ref, mass_ref, flags_ref, columns_ref, gather_ref, wall_ref,
    inverse_ref, walls_ref, field_ref, *trace_refs
):
    lows = []
    heads, crosses, backs, tails = [], [], [], []
    for e in range(CELLS):
        factor = factor_ref[e]
        left = factor[:, :HEAD]
        right = factor[:, HEAD:]
        left_t = left.T
        right_t = right.T
        scale = 1.0 / UNKNOWNS
        mass = mass_ref[e : e + 1, :]
        lows.append(jnp.min(mass, axis=1, keepdims=True))
        heads.append(scale * dot(left_t, left) + jnp.where(eye_mask(HEAD), mass[:, :HEAD], 0.0))
        crosses.append(scale * dot(left_t, right))
        backs.append(scale * dot(right_t, left))
        tails.append(scale * dot(right_t, right) + jnp.where(eye_mask(TAIL), mass[:, HEAD:], 0.0))
    firsts, ratios = approximate_inverses(heads, lows)
    first_parts = [halves(x) for x in firsts]
    carried = [dot_split(p, halves(c)) for p, c in zip(first_parts, crosses)]
    carried_parts = [halves(c) for c in carried]
    schurs = [
        tail - dot_split(halves(back), c) for tail, back, c in zip(tails, backs, carried_parts)
    ]
    lasts, more = approximate_inverses(schurs, lows)
    last_parts = [halves(x) for x in lasts]
    for e in range(CELLS):
        corner = -dot_split(carried_parts[e], last_parts[e])
        inverse_ref[e, HEAD:, HEAD:] = lasts[e]
        inverse_ref[e, :HEAD, HEAD:] = corner
        inverse_ref[e, HEAD:, :HEAD] = -dot_split(last_parts[e], carried_parts[e], dot_nt)
        inverse_ref[e, :HEAD, :HEAD] = firsts[e] - dot_split(halves(corner), carried_parts[e], dot_nt)
    worst = ratios[0]
    for ratio in ratios[1:] + more:
        worst = jnp.maximum(worst, ratio)

    @pl.when(jnp.logical_not(jnp.max(worst) <= CONDITION_LIMIT))
    def _():
        diagonal = eye_mask(UNKNOWNS)
        lane = lax.broadcasted_iota(jnp.int32, (1, UNKNOWNS), 1)
        line = lax.broadcasted_iota(jnp.int32, (UNKNOWNS, 1), 0)

        def element(e, carry):
            factor = factor_ref[e]
            mass = mass_ref[pl.ds(e, 1), :]
            inverse_ref[e] = dot(factor.T, factor) / UNKNOWNS + jnp.where(diagonal, mass, 0.0)

            def sweep(k, inner):
                table = inverse_ref[e]
                row = inverse_ref[e, pl.ds(k, 1), :]
                column = jnp.sum(jnp.where(diagonal, row, 0.0), axis=1, keepdims=True)
                pivot = jnp.sum(jnp.where(lane == k, row, 0.0), axis=1, keepdims=True)
                scaled = row / pivot
                swept = table - column * scaled
                swept = jnp.where(line == k, scaled, swept)
                swept = jnp.where(lane == k, column / pivot, swept)
                swept = jnp.where((line == k) & (lane == k), -1.0 / pivot, swept)
                inverse_ref[e] = swept
                return inner

            lax.fori_loop(0, UNKNOWNS, sweep, 0)
            inverse_ref[e] = -inverse_ref[e]
            return carry

        lax.fori_loop(0, CELLS, element, 0)

    walls_ref[...] = wall_weight * dot(flags_ref[...].astype(f32).astype(bf16), wall_ref[...])
    field = apply_inverses(inverse_ref, columns_ref[...])
    field_ref[...] = field
    store_traces(traces_of(field, gather_ref[...]), trace_refs)


def coupled(
    field_ref, walls_ref, flags_ref, face_ref, tops, own, received, scatter_ref
):
    lane8 = lax.broadcasted_iota(jnp.int32, (FACE, CELLS), 1)
    pieces = []
    for d, axis in enumerate(AXES):
        here = lax.axis_index(axis)
        has_below = here > 0
        has_above = here < lax.axis_size(axis) - 1
        upper = own[2 * d][...]
        lower = own[2 * d + 1][...]
        below = jnp.where(has_below, received[2 * d][...], 0.0)
        above = received[2 * d + 1][...]
        step = (CELLS, 2, 1)[d]
        count = (1, 4, 2)[d]
        upper_wide = jnp.concatenate([upper, jnp.zeros_like(upper)], axis=1)
        below_wide = jnp.concatenate([below, jnp.zeros_like(below)], axis=1)
        low_part = jnp.zeros((FACE, CELLS), f32)
        high_part = jnp.zeros((FACE, CELLS), f32)
        for e in range(CELLS):
            spot = (e // step) % count
            if spot == 0:
                other = e + step * (count - 1)
                left = below_wide[other : other + 1]
            else:
                left = upper_wide[e - step : e - step + 1]
            pair = left + lower[e : e + 1]
            flux = jnp.sum(face_ref[e, d] * pair[:, : 2 * FACE], axis=1, keepdims=True)
            closed = flags_ref[e, 2 * d] != 0
            flux = jnp.where(closed, 0.0, flux)
            low_part = jnp.where(lane8 == e, -flux, low_part)
            if spot > 0:
                high_part = jnp.where(lane8 == e - step, flux, high_part)
            if spot == count - 1:
                first = e - step * (count - 1)
                pair = upper_wide[e : e + 1] + above[first : first + 1]
                slot = (e, e - 6, e // 2)[d]
                flux = jnp.sum(tops[d][slot] * pair[:, : 2 * FACE], axis=1, keepdims=True)
                closed = flags_ref[e, 2 * d + 1] != 0
                flux = jnp.where(jnp.logical_and(jnp.logical_not(closed), has_above), flux, 0.0)
                high_part = jnp.where(lane8 == e, flux, high_part)
        pieces += [low_part, high_part]
    flux_columns = jnp.concatenate(pieces, axis=0)
    scatter = scatter_ref[...]
    high, middle, low = thirds(flux_columns)
    columns = dot(scatter, high) + (dot(scatter, middle) + dot(scatter, low))
    return columns + (walls_ref[...] * field_ref[...]).T


def split_refs(refs):
    own, received, tops = refs[:6], refs[6:12], refs[12:15]
    return own, received, tops, refs[15:]


def step_kernel(flags_ref, inverse_ref, walls_ref, gather_ref, scatter_ref, field_ref, face_ref, *refs):
    own, received, tops, outs = split_refs(refs)
    columns = coupled(field_ref, walls_ref, flags_ref, face_ref, tops, own, received, scatter_ref)
    outs[0][...] = columns
    field = apply_inverses(inverse_ref, columns)
    outs[1][...] = field
    store_traces(traces_of(field, gather_ref[...]), outs[2:])


def dots_kernel(flags_ref, walls_ref, scatter_ref, field_ref, face_ref, first_ref, second_ref, third_ref, *refs):
    own, received, tops, outs = split_refs(refs)
    last = coupled(field_ref, walls_ref, flags_ref, face_ref, tops, own, received, scatter_ref)
    vectors = [first_ref[...], second_ref[...], third_ref[...], last]
    lane = lax.broadcasted_iota(jnp.int32, (8, LANES), 1)
    packed = jnp.zeros((8, LANES), f32)
    for i in range(4):
        for j in range(i, 4):
            value = jnp.sum(jnp.sum(vectors[i] * vectors[j], axis=0, keepdims=True), axis=1, keepdims=True)
            packed = jnp.where(lane == 4 * i + j, value, packed)
    outs[0][...] = packed


def least_squares(columns, start_norm):
    count = len(columns)
    cosines = []
    sine_terms = []
    target_values = [start_norm] + [jnp.zeros_like(start_norm) for i in range(count)]
    triangle = []
    for j in range(count):
        column = list(columns[j])
        for i in range(j):
            first_entry = column[i]
            second_entry = column[i + 1]
            column[i] = cosines[i] * first_entry + sine_terms[i] * second_entry
            column[i + 1] = -sine_terms[i] * first_entry + cosines[i] * second_entry
        radius = jnp.sqrt(column[j] * column[j] + column[j + 1] * column[j + 1])
        cosine = column[j] / radius
        sine_part = column[j + 1] / radius
        cosines.append(cosine)
        sine_terms.append(sine_part)
        column[j] = radius
        target_values[j + 1] = -sine_part * target_values[j]
        target_values[j] = cosine * target_values[j]
        triangle.append(column[: j + 1])
    weights = [None] * count
    for i in reversed(range(count)):
        running = target_values[i]
        for k in range(i + 1, count):
            running = running - triangle[k][i] * weights[k]
        weights[i] = running / triangle[i][i]
    return weights


def finish_kernel(partial_ref, first_ref, second_ref, third_ref, out_ref):
    totals = jnp.sum(partial_ref[...], axis=0, keepdims=True)
    lane = lax.broadcasted_iota(jnp.int32, (1, LANES), 1)

    def entry(i, j):
        return jnp.sum(jnp.where(lane == 4 * i + j, totals, 0.0), axis=1, keepdims=True)

    upper = [[None] * 4 for i in range(4)]
    for i in range(4):
        for j in range(i, 4):
            value = entry(i, j)
            for k in range(i):
                value = value - upper[k][i] * upper[k][j]
            upper[i][j] = jnp.sqrt(value) if i == j else value / upper[i][i]
    columns = []
    for j in range(KRYLOV):
        column = []
        for i in range(j + 2):
            value = upper[i][j + 1]
            if i <= j:
                value = value + upper[i][j]
            column.append(value)
        columns.append(column)
    weights = least_squares(columns, upper[0][0])
    out_ref[...] = (
        weights[0] * first_ref[...] + weights[1] * second_ref[...] + weights[2] * third_ref[...]
    )


def vmem(count):
    return [pl.BlockSpec(memory_space=pltpu.VMEM)] * count


SMEM_SPEC = pl.BlockSpec(memory_space=pltpu.SMEM)


def call(kernel, specs, shapes, name, megabytes, args):
    return pl.pallas_call(
        kernel,
        out_shape=[jax.ShapeDtypeStruct(shape, f32) for shape in shapes],
        in_specs=specs,
        out_specs=vmem(len(shapes)),
        name=name,
        compiler_params=pltpu.CompilerParams(vmem_limit_bytes=megabytes << 20),
    )(*args)


TRACE_SHAPES = [(CELLS, LANES), (CELLS, 2 * LANES)] * 3


def around(block, axis, distance):
    count = lax.axis_size(axis)
    return lax.ppermute(block, axis, [(i, (i + distance) % count) for i in range(count)])


def exchanged(own):
    received = []
    for d, axis in enumerate(AXES):
        received.append(around(own[2 * d], axis, 1))
        received.append(around(own[2 * d + 1], axis, -1))
    return received


def shards(flux_jacobian_factor, mass_over_timestep, face_jacobian, face_flags, right_side):
    gather = jnp.asarray(gather_matrix(), bf16)
    scatter = jnp.asarray(scatter_matrix(), bf16)
    wall = jnp.asarray(wall_table(), bf16)
    flags = face_flags.reshape(CELLS, 6)
    faces = face_jacobian.reshape(CELLS, 3, FACE, 2 * FACE)
    tops = [
        around(face_jacobian[0:1, :, :, 0].reshape(8, FACE, 2 * FACE), "gx", -1),
        around(face_jacobian[:, 0:1, :, 1].reshape(2, FACE, 2 * FACE), "gy", -1),
        around(face_jacobian[:, :, 0:1, 2].reshape(4, FACE, 2 * FACE), "gz", -1),
    ]
    residual = right_side.reshape(CELLS, UNKNOWNS)
    vectors = [residual.T]
    inverse, walls, field, *own = call(
        invert_kernel,
        vmem(6),
        [(CELLS, UNKNOWNS, UNKNOWNS), (CELLS, UNKNOWNS), (CELLS, UNKNOWNS)] + TRACE_SHAPES,
        "invert",
        48,
        (
            flux_jacobian_factor.reshape(CELLS, UNKNOWNS, UNKNOWNS),
            mass_over_timestep.reshape(CELLS, UNKNOWNS),
            flags,
            vectors[0],
            gather,
            wall,
        ),
    )
    fields = [field]
    for j in range(KRYLOV - 1):
        received = exchanged(own)
        columns, field, *own = call(
            step_kernel,
            [SMEM_SPEC] + vmem(21),
            [(UNKNOWNS, CELLS), (CELLS, UNKNOWNS)] + TRACE_SHAPES,
            "step",
            24,
            (flags, inverse, walls, gather, scatter, fields[j], faces, *own, *received, *tops),
        )
        vectors.append(columns)
        fields.append(field)
    received = exchanged(own)
    (packed,) = call(
        dots_kernel,
        [SMEM_SPEC] + vmem(22),
        [(8, LANES)],
        "dots",
        24,
        (flags, walls, scatter, fields[2], faces, *vectors, *own, *received, *tops),
    )
    devices = lax.axis_size("gx") * lax.axis_size("gy") * lax.axis_size("gz")
    spread = jnp.broadcast_to(packed[0:1], (devices, LANES))
    partial = lax.all_to_all(spread, AXES, 0, 0, tiled=True)
    (update,) = call(
        finish_kernel, vmem(4), [(CELLS, UNKNOWNS)], "finish", 24, (partial, *fields)
    )
    return update.reshape(right_side.shape)


def solution(mesh):
    in_specs = (
        P("gx", "gy", "gz", None, None),
        P("gx", "gy", "gz", None),
        P("gx", "gy", "gz", None, None, None),
        P("gx", "gy", "gz", None),
        P("gx", "gy", "gz", None),
    )
    out_specs = P("gx", "gy", "gz", None)
    return jax.shard_map(shards, mesh=mesh, in_specs=in_specs, out_specs=out_specs, check_vma=False)
```

time: 1580 us -> 626 us (0.40)
  other arithmetic: 709 us -> 0 us
  blocking collectives: 535 us -> 20 us
  starting transfers between devices: 47.4 us -> 562 us
  local copies, waits for them, and re-layouts: 171 us -> 10.1 us
  matrix products: 87.4 us -> 0 us
  Pallas kernels: 0 us -> 18.4 us
    another operation x42 -> x0, other arithmetic: 651 us -> none  [the longest x14 394 us: shards(): factor_lower = jnp.linalg.cholesky(jacobian)]
    psum x7 -> x0, blocking collectives: 535 us -> none  [the longest x3 235 us: shards(): project = lax.psum(local_dots, ('gx', 'gy', 'gz'))]
    ppermute x21, starting transfers between devices: 47.4 us -> 562 us  [around(): lax.ppermute(block, axis, [(i, (i + distance) % count) for i in range(cou...]
    dot_general x27 -> x0, matrix products: 65.4 us -> none  [the longest x4 22.7 us: precond_apply(): jnp.einsum('abcij,abcj->abci', precond, vector, precision=full_precision)]
    another operation x77 -> x2, local copies, waits for them, and re-layouts: 62.7 us -> 2.39 us  [the longest x1 1.71 us: shards(): face_jacobian[:, :, 0:1, 2].reshape(4, FACE, 2 * FACE)]
    slice x57 -> x2, local copies, waits for them, and re-layouts: 38.4 us -> 2.12 us  [the longest x1 2.12 us: shards(): face_jacobian[0:1, :, :, 0].reshape(8, FACE, 2 * FACE)]
    another operation x9 -> x0, matrix products: 22 us -> none  [the longest x5 13.5 us: shards(): jax.scipy.linalg.solve_triangular(factor_lower, jnp.broadcast_to(identity...]
    add x24 -> x0, other arithmetic: 20.9 us -> none  [the longest x9 8.47 us: couple_faces(): return put_face(lower_part, d, 0) + put_face(upper_part, d, ORDER - 1)]
  transfers between devices with their start and end apart: 21 -> 21, of which waited for: 1 -> 8; matrix products, arithmetic and copies ran while one was open for 13% -> 0% of each run, Pallas kernels for 0% -> 2%
where the time goes in v1:
time: 626 us; the launch traced here: 625 us
  starting transfers between devices  562 us (90%)
  blocking collectives  20 us (3%)
  Pallas kernels  18.4 us (3%)
  waiting for transfers between devices  14.7 us (2%)
  local copies, waits for them, and re-layouts  10.1 us (2%)
    ppermute x21, starting transfers between devices, around(): lax.ppermute(block, axis, [(i, (i + distance) % count) for i in range(cou...  562 us
    all_to_all x1, blocking collectives, shards(): partial = lax.all_to_all(spread, AXES, 0, 0, tiled=True)  20 us
    pallas_call x5, Pallas kernels, call(): pl.pallas_call(kernel, out_shape=[jax.ShapeDtypeStruct(shape, f32) for sh...  18.4 us
    ppermute x21, waiting for transfers between devices, around(): lax.ppermute(block, axis, [(i, (i + distance) % count) for i in range(cou...  14.7 us
  transfers between devices with their start and end apart: 21, of which 8 were waited for; matrix products, arithmetic and copies ran while one was open for 0% of the time, Pallas kernels for 2%

profile of v1, /device:TPU:1, one launch (start us, length us, event | category | flops | bytes accessed | tf_op | source)
XLA Modules:
  0.0 625.5 jit_solution(333081636246381389)
XLA Ops:
  0.0 2.1 slice.14
  2.2 3.6 collective-permute-start.6
  5.7 1.7 slice_bitcast_fusion
  7.4 2.5 collective-permute-start.8
  13.1 1.5 copy-done.4
  14.7 11.0 %invert.1 = (f32[8,320,320]{2,1,0:T(8,128)}, f32[8,320]{1,0:T(8,128)S(1)}, f32[8,320]{1,0:T(8,128)S(1)}, f32[8,128]{1,0:T(8,128)S(1)}, f32[8,256]{1,0:T(8,128)S(...) custom-call(bf16[8,320,320]{2,1,0:T(8,128)(2,1)S(1)} %bitcast.19, ...), custom_call_target="tpu_custom_call" | custom-call | tf_op jit(solution)/shard_map/invert/pallas_call | solution.py:374
  25.7 1.5 collective-permute-start.2
  27.2 2.1 collective-permute-done.refs_6_
  29.4 533.5 %collective-permute-start.1 = (f32[8,256]{1,0:T(8,128)S(1)}, f32[8,256]{1,0:T(8,128)S(1)}, u32[]{:S(2)}, u32[]{:S(2)}) collective-permute-start(f32[8,256]{1,0:T(8,128)S(1)} %get-tuple-element.34.refs_1_), channel_id=1, source_target_pairs={{0,192},{64,0},{128,64},{192,128},{1,193},{65,1},{129,65},{193,129... | collective-permute-start | bytes 24584 | tf_op jit(solution)/shard_map/ppermute | solution.py:389
  562.8 4.4 collective-permute-done.4.refs_10_
  567.2 6.3 %collective-permute-start.3 = (f32[8,256]{1,0:T(8,128)S(1)}, f32[8,256]{1,0:T(8,128)S(1)}, u32[]{:S(2)}, u32[]{:S(2)}) collective-permute-start(f32[8,256]{1,0:T(8,128)S(1)} %get-tuple-element.36.refs_3_), channel_id=1, source_target_pairs={{0,60},{4,0},{8,4},{12,8},{16,12},{20,16},{24,20},{28,24},{32,28},... | collective-permute-start | bytes 24584 | tf_op jit(solution)/shard_map/ppermute | solution.py:389
  574.4 1.7 collective-permute-done.5.refs_11_
  576.1 2.1 copy-done.1
  578.2 2.6 step.2
  580.8 1.8 collective-permute-start.9
  583.5 2.7 collective-permute-start.12
  588.4 2.5 collective-permute-done.13.refs_10_
  590.9 2.6 step.3
  593.8 2.4 collective-permute-start.16
  596.3 2.3 collective-permute-start.18
  598.6 1.5 collective-permute-start.19
  600.4 2.2 collective-permute-done.19.refs_10_
  602.6 2.0 dots.1
  604.6 20.0 %all_to_all.8 = f32[256,1,128]{2,1,0:T(1,128)S(1)} all-to-all(f32[256,1,128]{2,1,0:T(1,128)S(1)} %broadcast_in_dim.2), channel_id=1, replica_groups=mesh['gx'=4,'gy'=16,'gz'=4] {'gx','gy','gz'}, dimensions={0} | all-to-all | bytes 262144 | tf_op jit(solution)/shard_map/all_to_all | solution.py:452
  (51 shorter events, 8.7 us)
Async XLA Ops:
  0.0 12.0 %copy-start.6 = (bf16[6,320]{1,0:T(8,128)(2,1)S(1)}, bf16[6,320]{1,0:T(8,128)(2,1)}, u32[]{:S(2)}) copy-start(bf16[6,320]{1,0:T(8,128)(2,1)} %constant.8.clone.wall_ref) | copy-start | bytes 11524
  0.0 12.0 %copy-start.5 = (s32[1,4,2,6]{3,2,1,0:T(2,128)S(1)}, s32[1,4,2,6]{3,2,1,0:T(2,128)}, u32[]{:S(2)}) copy-start(s32[1,4,2,6]{3,2,1,0:T(2,128)} %param.11) | copy-start | bytes 580
  2.2 573.9 %copy-start.3 = (bf16[320,480]{1,0:T(8,128)(2,1)S(1)}, bf16[320,480]{1,0:T(8,128)(2,1)}, u32[]{:S(2)}) copy-start(bf16[320,480]{1,0:T(8,128)(2,1)} %constant.7.clone.scatter_ref) | copy-start | bytes 921604
  2.2 573.9 %collective-permute-start.6 = (f32[8,80,160]{2,1,0:T(8,128)}, f32[8,80,160]{2,1,0:T(8,128)S(1)}, u32[]{:S(2)}, u32[]{:S(2)}) collective-permute-start(f32[8,80,160]{2,1,0:T(8,128)} %bitcast.4), channel_id=1, source_target_pairs={{0,192},{64,0},{128,64},{192,128},{1,193},{65,1},{129,65},{193,129... | collective-permute-start | bytes 1228808 | tf_op jit(solution)/shard_map/ppermute | solution.py:389
  7.4 568.6 %collective-permute-start.8 = (f32[4,80,160]{2,1,0:T(8,128)}, f32[4,80,160]{2,1,0:T(8,128)S(1)}, u32[]{:S(2)}, u32[]{:S(2)}) collective-permute-start(f32[4,80,160]{2,1,0:T(8,128)} %slice_bitcast_fusion), channel_id=1, source_target_pairs={{0,3},{1,0},{2,1},{3,2},{4,7},{5,4},{6,5},{7,6},{8,11},{9,8},{10,9... | collective-permute-start | bytes 614408 | tf_op jit(solution)/shard_map/ppermute | solution.py:389
  10.6 565.5 %collective-permute-start.7 = (f32[2,80,160]{2,1,0:T(8,128)}, f32[2,80,160]{2,1,0:T(8,128)}, u32[]{:S(2)}, u32[]{:S(2)}) collective-permute-start(f32[2,80,160]{2,1,0:T(8,128)} %slice_bitcast_fusion.1), channel_id=1, source_target_pairs={{0,60},{4,0},{8,4},{12,8},{16,12},{20,16},{24,20},{28,24},{32,28},... | collective-permute-start | bytes 307208 | tf_op jit(solution)/shard_map/ppermute | solution.py:389
  25.7 3.7 collective-permute-start
  25.7 537.1 %collective-permute-start.2 = (f32[8,128]{1,0:T(8,128)S(1)}, f32[8,128]{1,0:T(8,128)S(1)}, u32[]{:S(2)}, u32[]{:S(2)}) collective-permute-start(f32[8,128]{1,0:T(8,128)S(1)} %get-tuple-element.35.refs_2_), channel_id=1, source_target_pairs={{0,4},{4,8},{8,12},{12,16},{16,20},{20,24},{24,28},{28,32},{32,36}... | collective-permute-start | bytes 12296 | tf_op jit(solution)/shard_map/ppermute | solution.py:389
  29.4 544.2 %collective-permute-start.1 = (f32[8,256]{1,0:T(8,128)S(1)}, f32[8,256]{1,0:T(8,128)S(1)}, u32[]{:S(2)}, u32[]{:S(2)}) collective-permute-start(f32[8,256]{1,0:T(8,128)S(1)} %get-tuple-element.34.refs_1_), channel_id=1, source_target_pairs={{0,192},{64,0},{128,64},{192,128},{1,193},{65,1},{129,65},{193,129... | collective-permute-start | bytes 24584 | tf_op jit(solution)/shard_map/ppermute | solution.py:389
  562.8 4.4 collective-permute-start.4
  567.2 7.1 %collective-permute-start.3 = (f32[8,256]{1,0:T(8,128)S(1)}, f32[8,256]{1,0:T(8,128)S(1)}, u32[]{:S(2)}, u32[]{:S(2)}) collective-permute-start(f32[8,256]{1,0:T(8,128)S(1)} %get-tuple-element.36.refs_3_), channel_id=1, source_target_pairs={{0,60},{4,0},{8,4},{12,8},{16,12},{20,16},{24,20},{28,24},{32,28},... | collective-permute-start | bytes 24584 | tf_op jit(solution)/shard_map/ppermute | solution.py:389
  573.5 2.5 collective-permute-start.5
  580.8 6.4 %collective-permute-start.9 = (f32[8,128]{1,0:T(8,128)S(1)}, f32[8,128]{1,0:T(8,128)S(1)}, u32[]{:S(2)}, u32[]{:S(2)}) collective-permute-start(f32[8,128]{1,0:T(8,128)S(1)} %get-tuple-element.40.refs_0_), channel_id=1, source_target_pairs={{0,64},{64,128},{128,192},{192,0},{1,65},{65,129},{129,193},{193,1... | collective-permute-start | bytes 12296 | tf_op jit(solution)/shard_map/ppermute | solution.py:389
  582.6 8.2 %collective-permute-start.10 = (f32[8,256]{1,0:T(8,128)S(1)}, f32[8,256]{1,0:T(8,128)S(1)}, u32[]{:S(2)}, u32[]{:S(2)}) collective-permute-start(f32[8,256]{1,0:T(8,128)S(1)} %get-tuple-element.41.refs_1_), channel_id=1, source_target_pairs={{0,192},{64,0},{128,64},{192,128},{1,193},{65,1},{129,65},{193,129... | collective-permute-start | bytes 24584 | tf_op jit(solution)/shard_map/ppermute | solution.py:389
  583.5 7.3 %collective-permute-start.12 = (f32[8,256]{1,0:T(8,128)S(1)}, f32[8,256]{1,0:T(8,128)S(1)}, u32[]{:S(2)}, u32[]{:S(2)}) collective-permute-start(f32[8,256]{1,0:T(8,128)S(1)} %get-tuple-element.43.refs_3_), channel_id=1, source_target_pairs={{0,60},{4,0},{8,4},{12,8},{16,12},{20,16},{24,20},{28,24},{32,28},... | collective-permute-start | bytes 24584 | tf_op jit(solution)/shard_map/ppermute | solution.py:389
  586.2 4.7 collective-permute-start.14
  587.2 1.2 collective-permute-start.11
  587.2 3.7 collective-permute-start.13
  593.5 5.1 collective-permute-start.15
  593.8 8.7 %collective-permute-start.16 = (f32[8,256]{1,0:T(8,128)S(1)}, f32[8,256]{1,0:T(8,128)S(1)}, u32[]{:S(2)}, u32[]{:S(2)}) collective-permute-start(f32[8,256]{1,0:T(8,128)S(1)} %get-tuple-element.50.refs_1_), channel_id=1, source_target_pairs={{0,192},{64,0},{128,64},{192,128},{1,193},{65,1},{129,65},{193,129... | collective-permute-start | bytes 24584 | tf_op jit(solution)/shard_map/ppermute | solution.py:389
  596.3 6.3 %collective-permute-start.18 = (f32[8,256]{1,0:T(8,128)S(1)}, f32[8,256]{1,0:T(8,128)S(1)}, u32[]{:S(2)}, u32[]{:S(2)}) collective-permute-start(f32[8,256]{1,0:T(8,128)S(1)} %get-tuple-element.52.refs_3_), channel_id=1, source_target_pairs={{0,60},{4,0},{8,4},{12,8},{16,12},{20,16},{24,20},{28,24},{32,28},... | collective-permute-start | bytes 24584 | tf_op jit(solution)/shard_map/ppermute | solution.py:389
  598.6 4.0 collective-permute-start.20
  598.6 1.8 collective-permute-start.17
  598.6 4.0 collective-permute-start.19
  (6 other events, 38.3 us)
